TPU v7x, 256 devices: a whole 4x4x8 slice. The times are simulated.
256 devices in a mesh: req: 4 (over y), blk: 16 (over z, x_lo), tp: 4 (over x_hi, core).
Axes of the slice: x: 4 (x_hi: 2, x_lo: 2; x = x_hi * 2 + x_lo), y: 4, z: 8, core: 2. Of those that a mesh axis runs over, the one named last changes fastest.
Arguments:
- tokens: bfloat16 [4, 2048, 5120], P('req', 'blk', 'tp'), may hold values from -6 to 6
- gain: bfloat16 [5120], replicated, may hold values from 0.5 to 1.5
- w_query: bfloat16 [5120, 5120], P('req', 'tp'), may hold values from -0.078125 to 0.078125
- b_query: bfloat16 [5120], P('tp'), may hold values from -4 to 4
- w_keyval: bfloat16 [5120, 2, 1024], P('req', None, 'tp'), may hold values from -0.078125 to 0.078125
- b_keyval: bfloat16 [2, 1024], P(None, 'tp'), may hold values from -3 to 3
- kv_cache: bfloat16 [4, 2, 112, 128, 1024], P('req', None, 'blk', None, 'tp'), may hold values from -400 to 400
- cached_pages: int32 [4], P('req'), may hold values from 1 to 64, as said below
- page_table: int32 [4, 80], P('req'), may hold values from -1 to 111, as said below
Outputs:
- attended: bfloat16 [4, 2048, 5120], P('req', 'blk', 'tp')
- new_cache: bfloat16 [4, 2, 112, 128, 1024], P('req', None, 'blk', None, 'tp')
Inputs may be any that keep to these rules, and one draw needn't show every extreme that they name: `cached_pages`: one request has the most, 64. `page_table`: entry p of a request's row is the slot (owner index of blk times 7 plus slot) of its logical page p for p below its cached pages plus 16, and -1 beyond; the live pages of a request use distinct slots; one index of blk holds at most 4 cached pages of a request; the request with 64 cached pages has exactly 4 on every index of blk.
All inputs are finite; a program needn't handle non-finite values.
Results may differ from a plain program's by a relative error of at most 0.012.
The roundings to bfloat16 on the way count: a program that leaves them out, or rounds other values in their place, can miss the bound.
Values may be sent and summed in bfloat16 or wider, within the bound.
A program may use at most 128 MiB of HBM per device.

v0:
```python
import jax
import jax.numpy as jnp
from jax import lax
from jax.sharding import PartitionSpec as P

HEAD_SIZE = 128
PAGE_TOKENS = 128
epsilon = 1e-06
rope_base = 1000000.0


def normalize(inputs, gain):
    floats = inputs.astype(jnp.float32)
    scaling = lax.rsqrt(jnp.mean(floats * floats, axis=-1, keepdims=True) + epsilon)
    return (floats * scaling * gain.astype(jnp.float32)).astype(jnp.bfloat16)


def apply_rotation(vectors, token_positions):
    halfway = vectors.shape[-1] // 2
    frequency = rope_base ** (-(jnp.arange(halfway, dtype=jnp.float32) * 2.0 / vectors.shape[-1]))
    angles = token_positions[:, None] * frequency[None, :]
    cosine = jnp.cos(angles)[:, None, :]
    sine_part = jnp.sin(angles)[:, None, :]
    leading = vectors[..., :halfway]
    trailing = vectors[..., halfway:]
    return jnp.concatenate(
        [leading * cosine - trailing * sine_part, trailing * cosine + leading * sine_part], axis=-1
    )


def attend(running, query_rows_all, key_rows, value_rows, allowed):
    scaling = HEAD_SIZE ** (-0.5)
    scores = (
        jnp.einsum("rgjd,kgd->rgjk", query_rows_all, key_rows, preferred_element_type=jnp.float32)
        * scaling
    )
    scores = jnp.where(allowed[:, None, None, :], scores, -jnp.inf)
    maxima, totals, blended = running
    fresh_max = jnp.maximum(maxima, jnp.max(scores, axis=-1))
    weights = jnp.exp(scores - fresh_max[..., None])
    decays = jnp.exp(maxima - fresh_max)
    totals = totals * decays + jnp.sum(weights, axis=-1)
    blended = blended * decays[..., None] + jnp.einsum(
        "rgjk,kgd->rgjd",
        weights.astype(jnp.bfloat16),
        value_rows,
        preferred_element_type=jnp.float32,
    )
    return (fresh_max, totals, blended)


def make_fold(usable_all, query_rows_all, kv_heads_local, running, pieces):
    count = pieces.shape[1]
    stride = max((divisor for divisor in (4, 3, 2, 1) if count % divisor == 0))

    def advance(counter, carried):
        segment = lax.dynamic_slice_in_dim(pieces, counter * stride, stride, 1)
        usable = lax.dynamic_slice_in_dim(usable_all, counter * stride, stride)
        key_rows = segment[0].reshape(stride * PAGE_TOKENS, kv_heads_local, HEAD_SIZE)
        value_rows = segment[1].reshape(stride * PAGE_TOKENS, kv_heads_local, HEAD_SIZE)
        allowed = jnp.repeat(usable, PAGE_TOKENS)[None, :]
        return attend(carried, query_rows_all, key_rows, value_rows, allowed)

    return lax.fori_loop(0, count // stride, advance, running)


def body(tokens, gain, w_query, b_query, w_keyval, b_keyval, kv_cache, cached_pages, page_table):
    whole = lax.all_gather(tokens[0], "tp", axis=1, tiled=True)
    normed = normalize(whole, gain)
    rows_here = normed.shape[0]
    query_width = w_query.shape[1]
    kv_width = w_keyval.shape[2]
    pair_width = 2 * kv_width
    pieces = (
        lax.all_gather(w_query, "req", axis=0, tiled=True),
        lax.all_gather(w_keyval, "req", axis=0, tiled=True),
    )
    count = pieces[0].shape[0]
    query_sum = jnp.dot(normed, pieces[0], preferred_element_type=jnp.float32)
    pair_sum = jnp.dot(
        normed, pieces[1].reshape(count, pair_width), preferred_element_type=jnp.float32
    )
    length = cached_pages[0]
    page_map = page_table[0]
    own_index = lax.axis_index("blk")
    cycle_size = lax.axis_size("blk")
    heads_local = query_width // HEAD_SIZE
    kv_heads_local = kv_width // HEAD_SIZE
    queries_per_group = heads_local // kv_heads_local
    token_index = own_index * rows_here + jnp.arange(rows_here, dtype=jnp.int32)
    token_positions = (length * PAGE_TOKENS + token_index).astype(jnp.float32)
    query_full = query_sum + b_query.astype(jnp.float32)
    query_rows_all = apply_rotation(
        query_full.reshape(rows_here, heads_local, HEAD_SIZE), token_positions
    ).astype(jnp.bfloat16)
    query_rows_all = query_rows_all.reshape(rows_here, kv_heads_local, queries_per_group, HEAD_SIZE)
    pair_full = pair_sum + b_keyval.reshape(pair_width).astype(jnp.float32)
    fresh_key = apply_rotation(
        pair_full[:, :kv_width].reshape(rows_here, kv_heads_local, HEAD_SIZE), token_positions
    ).astype(jnp.bfloat16)
    fresh_value = pair_full[:, kv_width:].astype(jnp.bfloat16)
    fresh_pages = jnp.stack([fresh_key.reshape(rows_here, kv_width), fresh_value]).reshape(
        2, rows_here // PAGE_TOKENS, PAGE_TOKENS, kv_width
    )
    every_page = lax.all_gather(fresh_pages, "blk", axis=1, tiled=True)
    new_count = every_page.shape[1]
    fresh_rows = new_count * PAGE_TOKENS
    new_keys = every_page[0].reshape(fresh_rows, kv_heads_local, HEAD_SIZE)
    new_values = every_page[1].reshape(fresh_rows, kv_heads_local, HEAD_SIZE)
    allowed_fresh = jnp.arange(fresh_rows, dtype=jnp.int32)[None, :] <= token_index[:, None]
    starting = (
        jnp.full((rows_here, kv_heads_local, queries_per_group), -jnp.inf, jnp.float32),
        jnp.zeros((rows_here, kv_heads_local, queries_per_group), jnp.float32),
        jnp.zeros((rows_here, kv_heads_local, queries_per_group, HEAD_SIZE), jnp.float32),
    )
    running = attend(starting, query_rows_all, new_keys, new_values, allowed_fresh)
    cache_storage = kv_cache[0]
    slot_count = cache_storage.shape[1]
    new_slots = lax.dynamic_slice_in_dim(page_map, length, new_count)
    chooser = (
        new_slots[None, :]
        == own_index * slot_count + jnp.arange(slot_count, dtype=jnp.int32)[:, None]
    )
    written = jnp.einsum(
        "sj,cjpw->cspw",
        chooser.astype(jnp.bfloat16),
        every_page,
        preferred_element_type=jnp.float32,
    ).astype(jnp.bfloat16)
    landed = jnp.any(chooser, axis=1)
    new_storage = jnp.where(landed[None, :, None, None], written, cache_storage)
    pool_size = cycle_size * slot_count
    live = jnp.arange(page_map.shape[0], dtype=jnp.int32) < length
    matches = (page_map[None, :] == jnp.arange(pool_size, dtype=jnp.int32)[:, None]) & live[None, :]
    valid = jnp.any(matches, axis=1)
    running = make_fold(
        valid,
        query_rows_all,
        kv_heads_local,
        running,
        lax.all_gather(cache_storage, "blk", axis=1, tiled=True),
    )
    maxima, totals, blended = running
    result = (blended / totals[..., None]).reshape(rows_here, query_width).astype(jnp.bfloat16)
    return (result[None], new_storage[None])


def solution(mesh):
    return jax.shard_map(
        body,
        mesh=mesh,
        in_specs=(
            P("req", "blk", "tp"),
            P(),
            P("req", "tp"),
            P("tp"),
            P("req", None, "tp"),
            P(None, "tp"),
            P("req", None, "blk", None, "tp"),
            P("req"),
            P("req", None),
        ),
        out_specs=(P("req", "blk", "tp"), P("req", None, "blk", None, "tp")),
        check_vma=False,
    )
```

profile of v0, /device:TPU:35, one launch (start us, length us, event | category | flops | bytes accessed | tf_op | source)
XLA Modules:
  0.0 774.0 jit_solution(6554469855381495535)
XLA Ops:
  11.2 25.5 %all-gather.13.cloned.1.call-done = bf16[1,128,5120]{2,1,0:T(8,128)(2,1)} async-done(((bf16[1,128,1280]{2,1,0:T(8,128)(2,1)}), bf16[1,128,5120]{2,1,0:T(8,128)(2,1)}) %all-gather.13.cloned.1.call-update) | async-done | bytes 1310736 | tf_op jit(solution)/shard_map/all_gather | solution.py:68
  38.4 59.7 %all-gather.9.cloned.1.call-done = bf16[5120,2,256]{2,1,0:T(2,128)(2,1)} async-done(((bf16[1280,2,256]{2,1,0:T(2,128)(2,1)}), bf16[5120,2,256]{2,1,0:T(2,128)(2,1)}) %all-gather.9.cloned.1.call-update) | async-done | bytes 5242896 | tf_op jit(solution)/shard_map/all_gather | solution.py:76
  98.1 3.5 copy.82
  106.3 60.9 %all-gather.15.cloned.1.call-done = bf16[2,2048,256]{2,1,0:T(8,128)(2,1)} async-done(((bf16[2,128,256]{2,1,0:T(8,128)(2,1)}), bf16[2,2048,256]{2,1,0:T(8,128)(2,1)}) %all-gather.15.cloned.1.call-update) | async-done | bytes 2097168 | tf_op jit(solution)/shard_map/all_gather | solution.py:105
  170.7 3.5 fusion.40
  175.3 127.5 %all-gather.11.cloned.1.call-done = bf16[5120,1280]{1,0:T(8,128)(2,1)} async-done(((bf16[1280,1280]{1,0:T(8,128)(2,1)}), bf16[5120,1280]{1,0:T(8,128)(2,1)}) %all-gather.11.cloned.1.call-update) | async-done | bytes 13107216 | tf_op jit(solution)/shard_map/all_gather | solution.py:75
  302.8 6.6 convolution_add_fusion
  315.9 3.6 fusion.46
  319.4 299.3 %all-gather.17.cloned.1.call-done = bf16[1,2,112,128,256]{4,3,2,1,0:T(8,128)(2,1)} async-done(((bf16[1,2,7,128,256]{4,3,2,1,0:T(8,128)(2,1)}), bf16[1,2,112,128,256]{4,3,2,1,0:T(8,128)(2,1)}) %all-gather.17.cloned.1.call-update) | async-done | bytes 14680080 | tf_op jit(solution)/shard_map/all_gather | solution.py:141
  618.7 146.7 %while.17 = (s32[]{:T(128)}, f32[128,2,5]{0,2,1:T(8,128)S(1)}, f32[128,2,5]{0,2,1:T(8,128)S(1)}, f32[128,2,5,128]{0,3,2,1:T(8,128)}, pred[112]{0:T(512)(128)(4,1...) while((s32[]{:T(128)}, f32[128,2,5]{0,2,1:T(8,128)S(1)}, ...), condition=%wide.region_7.8_spmd, body=%wide.region_4.0_spmd.sunk | while | flops 343083520 | bytes 12208327 | solution.py:64
  626.5 2.7 fusion.76
  631.7 2.7 fusion.76
  636.9 2.7 fusion.76
  642.2 2.7 fusion.76
  647.4 2.7 fusion.76
  652.7 2.7 fusion.76
  657.9 2.7 fusion.76
  663.1 2.7 fusion.76
  668.4 2.7 fusion.76
  673.6 2.7 fusion.76
  678.9 2.7 fusion.76
  684.1 2.7 fusion.76
  689.3 2.7 fusion.76
  694.6 2.7 fusion.76
  699.8 2.7 fusion.76
  705.0 2.7 fusion.76
  710.3 2.7 fusion.76
  720.8 2.7 fusion.76
  731.2 2.7 fusion.76
  741.7 2.7 fusion.76
  752.2 2.7 fusion.76
  762.7 2.7 fusion.76
  (345 shorter events, 108.2 us)
Async XLA Ops:
  7.2 29.5 %all-gather.13.cloned.1.call-start = ((), (), s32[]{:S(2)}) async-start(), calls=%async_computation.2 | async-start | bytes 1638400 | tf_op jit(solution)/shard_map/all_gather | solution.py:68
  7.9 90.2 %all-gather.9.cloned.1.call-start = ((), (), s32[]{:S(2)}) async-start(), calls=%async_computation | async-start | bytes 6553600 | tf_op jit(solution)/shard_map/all_gather | solution.py:76
  8.6 158.6 %all-gather.15.cloned.1.call-start = ((), (), s32[]{:S(2)}) async-start(), calls=%async_computation.3 | async-start | bytes 2228224 | tf_op jit(solution)/shard_map/all_gather | solution.py:105
  98.1 3.5 copy-start
  102.6 2.4 copy-start.3
  102.6 2.5 copy-start.4
  103.8 199.0 %all-gather.11.cloned.1.call-start = ((), (), s32[]{:S(2)}) async-start(), calls=%async_computation.1 | async-start | bytes 16384000 | tf_op jit(solution)/shard_map/all_gather | solution.py:75
  104.4 514.3 %all-gather.17.cloned.1.call-start = ((), (), s32[]{:S(2)}) async-start(), calls=%async_computation.4 | async-start | bytes 15597568 | tf_op jit(solution)/shard_map/all_gather | solution.py:141
  309.5 2.6 copy-start.2
  309.7 2.4 copy-start.1
Sparse Core Ops, SparseCore 0:
  9.8 26.8 all-gather.12
  38.5 59.5 all-gather.8
  104.0 63.2 all-gather.14
  168.9 133.8 all-gather.10
  304.5 314.2 all-gather.16
where the time goes:
time: 776 us; the launch traced here: 774 us
  waiting for transfers between devices  575 us (74%)
  matrix products  107 us (14%)
  local copies, waits for them, and re-layouts  48.8 us (6%)
  other arithmetic  26.9 us (3%)
  between operations  14.7 us (2%)
    all_gather x1, waiting for transfers between devices, body(): lax.all_gather(cache_storage, 'blk', axis=1, tiled=True)  299 us
    all_gather x1, waiting for transfers between devices, body(): lax.all_gather(w_query, 'req', axis=0, tiled=True)  127 us
    dot_general x29, matrix products, attend(): jnp.einsum('rgjk,kgd->rgjd', weights.astype(jnp.bfloat16), value_rows, pr...  79.7 us
    all_gather x1, waiting for transfers between devices, body(): every_page = lax.all_gather(fresh_pages, 'blk', axis=1, tiled=True)  60.9 us
    all_gather x1, waiting for transfers between devices, body(): lax.all_gather(w_keyval, 'req', axis=0, tiled=True)  59.7 us
    slice x28, local copies, waits for them, and re-layouts, advance(): segment[1].reshape(stride * PAGE_TOKENS, kv_heads_local, HEAD_SIZE)  29.8 us
    all_gather x1, waiting for transfers between devices, body(): whole = lax.all_gather(tokens[0], 'tp', axis=1, tiled=True)  25.5 us
    reduce_sum x29, other arithmetic, attend(): totals = totals * decays + jnp.sum(weights, axis=-1)  18.7 us
  transfers between devices with their start and end apart: 5, of which 5 were waited for; matrix products, arithmetic and copies ran while one was open for 4% of the time, Pallas kernels for 0%

commit v1 on v0

--- a/solution.py
+++ b/solution.py
@@ -7,6 +7,22 @@
 PAGE_TOKENS = 128
 epsilon = 1e-06
 rope_base = 1000000.0
+
+
+def collect(x, axis, dim):
+    ways, here, lap = (lax.axis_size(axis), lax.axis_index(axis), x.shape[dim])
+    shape = [n * ways if d == dim else n for d, n in enumerate(x.shape)]
+    full = lax.dynamic_update_slice_in_dim(jnp.zeros(shape, x.dtype), x, here * lap, axis=dim)
+    going_up = going_down = x
+    for far in range(1, ways // 2 + 1):
+        going_up = lax.ppermute(going_up, axis, [(d, (d + 1) % ways) for d in range(ways)])
+        full = lax.dynamic_update_slice_in_dim(full, going_up, (here - far) % ways * lap, axis=dim)
+        if 2 * far < ways:
+            going_down = lax.ppermute(going_down, axis, [(d, (d - 1) % ways) for d in range(ways)])
+            full = lax.dynamic_update_slice_in_dim(
+                full, going_down, (here + far) % ways * lap, axis=dim
+            )
+    return full
 
 
 def normalize(inputs, gain):
@@ -71,10 +87,7 @@
     query_width = w_query.shape[1]
     kv_width = w_keyval.shape[2]
     pair_width = 2 * kv_width
-    pieces = (
-        lax.all_gather(w_query, "req", axis=0, tiled=True),
-        lax.all_gather(w_keyval, "req", axis=0, tiled=True),
-    )
+    pieces = (collect(w_query, "req", 0), lax.all_gather(w_keyval, "req", axis=0, tiled=True))
     count = pieces[0].shape[0]
     query_sum = jnp.dot(normed, pieces[0], preferred_element_type=jnp.float32)
     pair_sum = jnp.dot(

time: 776 us -> 648 us (0.84)
  waiting for transfers between devices: 575 us -> 425 us
  local copies, waits for them, and re-layouts: 48.8 us -> 68.5 us
    all_gather x1 -> x0, waiting for transfers between devices: 127 us -> none  [body(): lax.all_gather(w_query, 'req', axis=0, tiled=True)]
    ppermute x0 -> x3, waiting for transfers between devices: none -> 124 us  [the longest x2 124 us: collect(): lax.ppermute(going_up, axis, [(d, (d + 1) % ways) for d in range(ways)])]
    all_gather x1, waiting for transfers between devices: 299 us -> 214 us  [body(): lax.all_gather(cache_storage, 'blk', axis=1, tiled=True)]
    all_gather x1, waiting for transfers between devices: 60.9 us -> 0.02 us  [body(): every_page = lax.all_gather(fresh_pages, 'blk', axis=1, tiled=True)]
    dynamic_update_slice x0 -> x4, local copies, waits for them, and re-layouts: none -> 15.6 us  [the longest x2 7.96 us: collect(): lax.dynamic_update_slice_in_dim(full, going_up, (here - far) % ways * lap...]
  transfers between devices with their start and end apart: 5 -> 7, of which waited for: 5 -> 5; matrix products, arithmetic and copies ran while one was open for 4% -> 8% of each run, Pallas kernels for 0% -> 0%
where the time goes in v1:
time: 648 us; the launch traced here: 646 us
  waiting for transfers between devices  425 us (66%)
  matrix products  107 us (17%)
  local copies, waits for them, and re-layouts  68.5 us (11%)
  other arithmetic  26.2 us (4%)
  between operations  14.7 us (2%)
    all_gather x1, waiting for transfers between devices, body(): lax.all_gather(cache_storage, 'blk', axis=1, tiled=True)  214 us
    ppermute x2, waiting for transfers between devices, collect(): lax.ppermute(going_up, axis, [(d, (d + 1) % ways) for d in range(ways)])  124 us
    dot_general x29, matrix products, attend(): jnp.einsum('rgjk,kgd->rgjd', weights.astype(jnp.bfloat16), value_rows, pr...  79.8 us
    all_gather x1, waiting for transfers between devices, body(): lax.all_gather(w_keyval, 'req', axis=0, tiled=True)  59.7 us
    slice x28, local copies, waits for them, and re-layouts, advance(): segment[1].reshape(stride * PAGE_TOKENS, kv_heads_local, HEAD_SIZE)  29.8 us
    all_gather x1, waiting for transfers between devices, body(): whole = lax.all_gather(tokens[0], 'tp', axis=1, tiled=True)  25.5 us
    reduce_sum x29, other arithmetic, attend(): totals = totals * decays + jnp.sum(weights, axis=-1)  18.7 us
    dot_general x29, matrix products, attend(): jnp.einsum('rgjd,kgd->rgjk', query_rows_all, key_rows, preferred_element_...  16.1 us
  transfers between devices with their start and end apart: 7, of which 5 were waited for; matrix products, arithmetic and copies ran while one was open for 8% of the time, Pallas kernels for 0%

profile of v1, /device:TPU:35, one launch (start us, length us, event | category | flops | bytes accessed | tf_op | source)
XLA Modules:
  0.0 645.7 jit_solution(1142708359110865976)
XLA Ops:
  11.2 25.5 %all-gather.10.cloned.1.call-done = bf16[1,128,5120]{2,1,0:T(8,128)(2,1)} async-done(((bf16[1,128,1280]{2,1,0:T(8,128)(2,1)}), bf16[1,128,5120]{2,1,0:T(8,128)(2,1)}) %all-gather.10.cloned.1.call-update) | async-done | bytes 1310736 | tf_op jit(solution)/shard_map/all_gather | solution.py:84
  38.4 59.7 %all-gather.8.cloned.1.call-done = bf16[5120,2,256]{2,1,0:T(2,128)(2,1)} async-done(((bf16[1280,2,256]{2,1,0:T(2,128)(2,1)}), bf16[5120,2,256]{2,1,0:T(2,128)(2,1)}) %all-gather.8.cloned.1.call-update) | async-done | bytes 5242896 | tf_op jit(solution)/shard_map/all_gather | solution.py:90
  98.1 3.5 copy.82
  107.2 70.6 %collective-permute-done = bf16[1280,1280]{1,0:T(8,128)(2,1)} collective-permute-done((bf16[1280,1280]{1,0:T(8,128)(2,1)}, bf16[1280,1280]{1,0:T(8,128)(2,1)}, u32[]{:S(2)}, u32[]{:S(2)}) %collective-permute-start) | collective-permute-done | bytes 3276832 | tf_op jit(solution)/shard_map/ppermute | solution.py:18
  179.1 5.7 broadcast_in_dim.99
  184.8 3.8 constant_dynamic-update-slice_fusion.3
  188.6 4.1 constant_dynamic-update-slice_fusion.2
  192.7 3.8 constant_dynamic-update-slice_fusion.1
  196.5 53.7 %collective-permute-done.2 = bf16[1280,1280]{1,0:T(8,128)(2,1)} collective-permute-done((bf16[1280,1280]{1,0:T(8,128)(2,1)}, bf16[1280,1280]{1,0:T(8,128)(2,1)}, u32[]{:S(2)}, u32[]{:S(2)}) %collective-permute-start.2) | collective-permute-done | bytes 3276832 | tf_op jit(solution)/shard_map/ppermute | solution.py:18
  250.2 3.8 constant_dynamic-update-slice_fusion
  254.0 6.7 %convolution_add_fusion = f32[128,1280]{1,0:T(8,128)S(1)} fusion(bf16[5120,1280]{1,0:T(8,128)(2,1)} %constant_dynamic-update-slice_fusion, bf16[1,128,5120]{2,1,0:T(8,128)(2,1)S(1)} %copy-done, f32[5120]{0:T(1024)S(1)} %convert_element_type.74, f32[128]{0:T(128)S(1)} %add_rsqrt_fusion, f32[1280]{0:T(1024)S(1)} %convert_element_type.80), kind=kOutput, calls=%fused_computation.35 | convolution fusion | flops 1680506880 | bytes 15099392 | tf_op jit(solution)/shard_map/dot_general | solution.py:92
  264.6 3.5 fusion.40
  273.1 3.6 fusion.46
  276.7 213.7 %all-gather.14.cloned.1.call-done = bf16[1,2,112,128,256]{4,3,2,1,0:T(8,128)(2,1)} async-done(((bf16[1,2,7,128,256]{4,3,2,1,0:T(8,128)(2,1)}), bf16[1,2,112,128,256]{4,3,2,1,0:T(8,128)(2,1)}) %all-gather.14.cloned.1.call-update) | async-done | bytes 14680080 | tf_op jit(solution)/shard_map/all_gather | solution.py:154
  490.4 146.7 %while.17 = (s32[]{:T(128)}, f32[128,2,5]{0,2,1:T(8,128)S(1)}, f32[128,2,5]{0,2,1:T(8,128)S(1)}, f32[128,2,5,128]{0,3,2,1:T(8,128)}, pred[112]{0:T(512)(128)(4,1...) while((s32[]{:T(128)}, f32[128,2,5]{0,2,1:T(8,128)S(1)}, ...), condition=%wide.region_7.8_spmd, body=%wide.region_4.7_spmd.sunk | while | flops 343083520 | bytes 12208327 | solution.py:80
  492.9 2.7 fusion.77
  498.2 2.7 fusion.77
  508.6 2.7 fusion.77
  513.9 2.7 fusion.77
  524.3 2.7 fusion.77
  529.6 2.7 fusion.77
  540.1 2.7 fusion.77
  545.3 2.7 fusion.77
  555.8 2.7 fusion.77
  561.0 2.7 fusion.77
  571.5 2.7 fusion.77
  576.7 2.7 fusion.77
  592.4 2.7 fusion.77
  602.9 2.7 fusion.77
  608.2 2.7 fusion.77
  618.6 2.7 fusion.77
  634.3 2.7 fusion.77
  (351 shorter events, 121.7 us)
Async XLA Ops:
  7.2 29.5 %all-gather.10.cloned.1.call-start = ((), (), s32[]{:S(2)}) async-start(), calls=%async_computation.1 | async-start | bytes 1638400 | tf_op jit(solution)/shard_map/all_gather | solution.py:84
  7.9 90.2 %all-gather.8.cloned.1.call-start = ((), (), s32[]{:S(2)}) async-start(), calls=%async_computation | async-start | bytes 6553600 | tf_op jit(solution)/shard_map/all_gather | solution.py:90
  8.6 253.1 %all-gather.12.cloned.1.call-start = ((), (), s32[]{:S(2)}) async-start(), calls=%async_computation.2 | async-start | bytes 2228224 | tf_op jit(solution)/shard_map/all_gather | solution.py:118
  98.1 3.5 copy-start
  102.5 75.3 %copy-start.2 = (bf16[1280]{0:T(1024)(128)(2,1)S(1)}, bf16[1280]{0:T(1024)(128)(2,1)}, u32[]{:S(2)}) copy-start(bf16[1280]{0:T(1024)(128)(2,1)} %param.14) | copy-start | bytes 7684
  102.5 75.4 %copy-start.3 = (s32[1,80]{1,0:T(1,128)S(1)}, s32[1,80]{1,0:T(1,128)}, u32[]{:S(2)}) copy-start(s32[1,80]{1,0:T(1,128)} %param.19) | copy-start | bytes 964
  103.8 386.6 %all-gather.14.cloned.1.call-start = ((), (), s32[]{:S(2)}) async-start(), calls=%async_computation.3 | async-start | bytes 15597568 | tf_op jit(solution)/shard_map/all_gather | solution.py:154
  104.4 73.4 %collective-permute-start = (bf16[1280,1280]{1,0:T(8,128)(2,1)}, bf16[1280,1280]{1,0:T(8,128)(2,1)}, u32[]{:S(2)}, u32[]{:S(2)}) collective-permute-start(bf16[1280,1280]{1,0:T(8,128)(2,1)} %param.13), channel_id=1, source_target_pairs={{0,64},{64,128},{128,192},{192,0},{1,65},{65,129},{129,193},{193,1... | collective-permute-start | bytes 9830408 | tf_op jit(solution)/shard_map/ppermute | solution.py:18
  105.2 87.5 %collective-permute-start.1 = (bf16[1280,1280]{1,0:T(8,128)(2,1)}, bf16[1280,1280]{1,0:T(8,128)(2,1)}, u32[]{:S(2)}, u32[]{:S(2)}) collective-permute-start(bf16[1280,1280]{1,0:T(8,128)(2,1)} %param.13), channel_id=1, source_target_pairs={{0,192},{64,0},{128,64},{192,128},{1,193},{65,1},{129,65},{193,129... | collective-permute-start | bytes 9830408 | tf_op jit(solution)/shard_map/ppermute | solution.py:21
  177.8 72.4 %collective-permute-start.2 = (bf16[1280,1280]{1,0:T(8,128)(2,1)}, bf16[1280,1280]{1,0:T(8,128)(2,1)}, u32[]{:S(2)}, u32[]{:S(2)}) collective-permute-start(bf16[1280,1280]{1,0:T(8,128)(2,1)} %collective-permute-done), channel_id=1, source_target_pairs={{0,64},{64,128},{128,192},{192,0},{1,65},{65,129},{129,193},{193,1... | collective-permute-start | bytes 9830408 | tf_op jit(solution)/shard_map/ppermute | solution.py:18
  264.6 4.7 copy-start.1
Sparse Core Ops, SparseCore 0:
  9.8 26.8 all-gather.9
  38.5 59.5 all-gather.7
  104.0 62.9 all-gather.11
  168.6 321.7 all-gather.13
